TPU v7x, 256 devices: a whole 4x4x8 slice. The times are simulated.
256 devices in a mesh: mem: 8 (over y, x_lo), grid: 32 (over x_hi, z, core).
Axes of the slice: x: 4 (x_hi: 2, x_lo: 2; x = x_hi * 2 + x_lo), y: 4, z: 8, core: 2. Of those that a mesh axis runs over, the one named last changes fastest.
Arguments:
- initial_concentrations: float32 [32, 4, 768, 1536], P('mem', None, 'grid'), may hold values from 0.5 to 2
- rate_field: bfloat16 [12, 768, 1536], P(None, 'grid'), may hold values from 0.019897461 to 0.29882812
- kinetic_scaling_factors: bfloat16 [32, 12, 256, 6], P('mem', None, 'grid'), may hold values from 0.5 to 2
- observed_cell: int32 [256, 6, 128], P('grid'), may hold values from 0 to 3071
- measured_value: float32 [256, 6, 128], P('grid'), may hold values from 0.5 to 2
- error_variance: float32 [256, 6, 128], P('grid'), may hold values from 0.05 to 0.5
Outputs:
- analysis: bfloat16 [32, 4, 768, 1536], P('mem', None, 'grid')
- mult_analysis: bfloat16 [32, 12, 256, 6], P('mem', None, 'grid')
Inputs may be any that keep to these rules, and one draw needn't show every extreme that they name: `observed_cell`: an observation's entry is tracer * 3 * 256 + row * 256 + column within its patch.
All inputs are finite; a program needn't handle non-finite values.
Results may differ from a plain program's by a relative error of at most 0.011.
The roundings to bfloat16 on the way count: a program that leaves them out, or rounds other values in their place, can miss the bound.
Values may be sent and summed in bfloat16 or wider, within the bound.
A program may use at most 64 MiB of HBM per device.

v0:
```python
import functools
import math

import jax
import jax.numpy as jnp
import ml_dtypes
import numpy as np
from jax import lax
from jax.experimental import pallas as pl
from jax.experimental.pallas import tpu as pltpu
from jax.sharding import PartitionSpec as P

NLAT = 768
NLON = 1536
NW = 512
PLAT = 3
PLON = 256
SWEEPS = 5
TRACERS = 4
MEMBERS = 32
REACTIONS = 12
DAMPING = 2.0

GROUPS = 8
BANDS = 32
LOCAL = 4
BLOCKS = 8
BAND = NLAT // BANDS
PATCHES = NLON // PLON
ROWS = TRACERS * PLAT
MESH = pl.DeviceIdType.MESH
HI = lax.Precision.HIGHEST
ZSTEPS = (4, 3, 5, 2, 6, 1, 7, 0)
PAIRS = ((1, 1), (0, 1), (1, 0), (0, 0))

f32 = jnp.float32
bf16 = jnp.bfloat16


def wave_numbers():
    block = np.arange(BLOCKS)[:, None]
    place = np.arange(NW // BLOCKS)[None, :]
    return 2 * ((block // 2) * (NW // BLOCKS) + place) + block % 2


@functools.lru_cache(maxsize=1)
def tables():
    waves = wave_numbers()
    m = waves.reshape(-1)
    phase = (m[:, None] * np.arange(NLON)[None, :]) % NLON
    angle = phase.astype(np.float32) * np.float32(2.0 * math.pi / NLON)
    cosine, sine = np.cos(angle), np.sin(angle)
    forward = np.stack([cosine, -sine], axis=1).reshape(2 * NW, NLON).T
    forward = forward.reshape(NLON, 4, 256).transpose(1, 0, 2)
    weight = np.where(m == 0, 1.0, 2.0).astype(np.float32)[:, None]
    inverse = np.stack([weight * cosine, -weight * sine], axis=1).reshape(2 * NW, NLON)
    inverse = inverse.reshape(2 * NW, PATCHES, PLON).transpose(1, 0, 2)

    order = np.arange(NW, dtype=np.float32)
    theta = (np.arange(NLAT, dtype=np.float32) + np.float32(0.5)) * np.float32(math.pi / NLAT)
    even = np.cos(theta[:, None] * order[None, :])
    odd = np.sin(theta[:, None] * (order[None, :] + np.float32(1.0)))
    both = np.stack([even, odd])
    to_modes = both.transpose(0, 2, 1)
    dest = np.arange(GROUPS)[:, None, None], np.arange(BANDS)[None, :, None], np.arange(PLAT)
    rows = (dest[1] * BAND + dest[0] * PLAT + dest[2]).reshape(-1)
    to_rows = both[:, rows, :]

    total = (waves[:, None, :] + np.arange(NW)[None, :, None]).astype(np.float32)
    ratio = total * (total + np.float32(1.0)) / np.float32(NW * (NW - 1))
    half = np.where((waves[:, None, :] % 2 == 0) & (np.arange(NW)[None, :, None] == 0), 0.5, 1.0)
    gain = (half / (1.0 + DAMPING * ratio * ratio)).astype(np.float32) * np.float32(2.0 / NLAT)
    gain = np.where(total <= NW - 1, gain, 0.0).astype(np.float32)
    gain = np.repeat(gain, 2, axis=2)

    spread = np.zeros((BANDS, 16, TRACERS, BANDS, PLAT), np.float32)
    for b in range(BANDS):
        for t in range(TRACERS):
            for j in range(PLAT):
                spread[b, t * PLAT + j, t, b, j] = 1.0
    spread = spread.reshape(BANDS * 16, TRACERS * BANDS * PLAT)
    gather = np.zeros((ROWS, MEMBERS, MEMBERS, 16), np.float32)
    for e in range(MEMBERS):
        for a in range(ROWS):
            gather[a, e, e, a] = 1.0
    gather = gather.reshape(ROWS * MEMBERS, MEMBERS * 16)
    home = np.zeros((GROUPS, LOCAL, ROWS, ROWS, GROUPS, LOCAL), np.float32)
    for g in range(GROUPS):
        for e in range(LOCAL):
            for a in range(ROWS):
                home[g, e, a, a, g, e] = 1.0
    home = home.reshape(MEMBERS * ROWS, ROWS * MEMBERS)
    b = lambda v: np.asarray(v, np.float32).astype(ml_dtypes.bfloat16)
    return b(forward), b(inverse), b(to_modes), b(to_rows), gain, b(spread), b(gather), b(home)


def split_grid(b):
    return b // 16, lax.rem(b // 2, 8), lax.rem(b, 2)


def peer(group_step, a, dz, c):
    g, b = lax.axis_index("mem"), lax.axis_index("grid")
    half, z, core = split_grid(b)
    band = lax.rem(half + a, 2) * 16 + lax.rem(z + dz, 8) * 2 + lax.rem(core + c, 2)
    return lax.rem(g + group_step, GROUPS), band


def kernel(
    x_hbm,
    fac,
    cells,
    measured,
    variance,
    field_hbm,
    forward_hbm,
    inverse_hbm,
    modes_hbm,
    rows_hbm,
    gain_hbm,
    spread_hbm,
    gather_hbm,
    home_hbm,
    out_hbm,
    mult_out,
    x,
    xb,
    forward,
    inverse,
    modes,
    rows,
    gain,
    spread,
    gather,
    home,
    field,
    field_rows,
    send1,
    recv1,
    staged,
    plane,
    damped,
    send2,
    recv2,
    padded,
    coefficients,
    fac_in,
    fac_wide,
    background,
    weighted,
    spread_seen,
    projected,
    transform,
    send3,
    mult_send,
    mult_in,
    load_sem,
    local_sem,
    send_sem,
    recv_sem,
):
    g, b = lax.axis_index("mem"), lax.axis_index("grid")
    half, z, core = split_grid(b)
    member = half * 2 + core

    def load(src, dst, i):
        return pltpu.make_async_copy(src, dst, load_sem.at[i])

    load_x = load(x_hbm, x, 0)
    load_x.start()
    load_forward = [load(forward_hbm.at[i], forward.at[i], 1 + i) for i in range(4)]
    for one in load_forward:
        one.start()
    parity = lax.rem(z, 2)
    later = [
        load(modes_hbm.at[parity], modes, 5),
        load(rows_hbm.at[parity], rows, 6),
        load(gain_hbm.at[z], gain, 7),
        load(spread_hbm, spread, 8),
        load(field_hbm, field, 9),
        load(inverse_hbm, inverse, 10),
        load(gather_hbm, gather, 11),
        load(home_hbm, home, 12),
    ]
    for one in later:
        one.start()

    barrier = pltpu.get_barrier_semaphore()

    def greet(step, carry):
        for a, c in PAIRS:
            for dz in ZSTEPS:

                def signal():
                    pl.semaphore_signal(
                        barrier, inc=1, device_id=peer(step, a, dz, c), device_id_type=MESH
                    )

                if a or c or dz:
                    signal()
                else:
                    pl.when(step != 0)(signal)
        return carry

    lax.fori_loop(0, GROUPS, greet, 0)

    load_x.wait()
    xb[...] = x[...].reshape(LOCAL * TRACERS * BAND, NLON).astype(bf16)
    for one in load_forward:
        one.wait()

    def forward_step(i, carry):
        value = jnp.dot(xb[...], forward[i], preferred_element_type=f32) * (1.0 / NLON)
        value = value.astype(bf16).reshape(LOCAL, TRACERS * BAND, 256)
        send1[2 * i] = value[:, :, :128]
        send1[2 * i + 1] = value[:, :, 128:]
        return carry

    lax.fori_loop(0, 4, forward_step, 0)
    pl.semaphore_wait(barrier, GROUPS * BANDS - 1)

    def remote(src, dst, i, to):
        return pltpu.make_async_remote_copy(
            src_ref=src,
            dst_ref=dst,
            send_sem=send_sem.at[i],
            recv_sem=recv_sem.at[i],
            device_id=to,
            device_id_type=MESH,
        )

    def wait_bytes(ref, sem):
        pltpu.make_async_copy(ref, ref, sem).wait()

    for a, c in PAIRS:
        for dz in ZSTEPS:
            if a or c or dz:
                _, band = peer(0, a, dz, c)
                h2, z2, c2 = split_grid(band)
                remote(send1.at[z2, h2 * 2 + c2], recv1.at[b], 0, (g, band)).start()
    own1 = pltpu.make_async_copy(send1.at[z, member], recv1.at[b], local_sem.at[0])
    own1.start()
    for step in range(1, GROUPS):
        to = lax.rem(g + step, GROUPS)
        remote(fac.at[to], fac_in.at[g], 1, (to, b)).start()
    own_fac = pltpu.make_async_copy(fac.at[g], fac_in.at[g], local_sem.at[1])
    own_fac.start()

    for one in later:
        one.wait()
    padded[...] = jnp.zeros(padded.shape, f32)

    line_of = lax.broadcasted_iota(jnp.int32, (8, BAND), 0) + g * PLAT
    own_lines = jnp.where(line_of == lax.broadcasted_iota(jnp.int32, (8, BAND), 1), 1.0, 0.0)
    own_lines = own_lines.astype(bf16)

    def widen(r, carry):
        field_rows[r] = jnp.dot(own_lines, field[r], preferred_element_type=f32)
        return carry

    lax.fori_loop(0, REACTIONS, widen, 0)
    own_fac.wait()
    wait_bytes(fac_in.at[pl.ds(0, GROUPS - 1)], recv_sem.at[1])
    wait_bytes(fac.at[pl.ds(0, GROUPS - 1)], send_sem.at[1])
    row_of = lax.broadcasted_iota(jnp.int32, (MEMBERS, GROUPS * 8), 0)
    col_of = lax.broadcasted_iota(jnp.int32, (MEMBERS, GROUPS * 8), 1)
    pick = jnp.where(col_of == (row_of // LOCAL) * 8 + lax.rem(row_of, LOCAL), 1.0, 0.0)
    factors = jnp.dot(
        pick.astype(bf16),
        fac_in[...].reshape(GROUPS * 8, 128).astype(bf16),
        preferred_element_type=f32,
    )
    for c in range(PATCHES):
        for r in range(REACTIONS):
            lane = c * REACTIONS + r
            fac_wide[c, r] = jnp.broadcast_to(factors[:, lane : lane + 1], (MEMBERS, 128))
    log_rate = jnp.log(factors)
    log_mean = jnp.mean(log_rate, axis=0, keepdims=True)
    log_spread = log_rate - log_mean

    own1.wait()
    wait_bytes(recv1.at[pl.ds(0, BANDS - 1)], recv_sem.at[0])

    def unpack(s, carry):
        value = recv1[s].astype(f32)
        at = pl.ds(pl.multiple_of(s * BAND, 8), BAND)
        for t in range(TRACERS):
            staged[at, t * 128 : (t + 1) * 128] = value[t * BAND : (t + 1) * BAND]
        return carry

    lax.fori_loop(0, BANDS, unpack, 0)
    plane[...] = staged[...].astype(bf16)

    def to_modes(i, carry):
        at = pl.ds(pl.multiple_of(i * 128, 128), 128)
        value = jnp.dot(modes[at, :], plane[...], preferred_element_type=f32)
        scale = gain[at, :]
        for t in range(TRACERS):
            lanes = slice(t * 128, (t + 1) * 128)
            damped[at, lanes] = (value[:, lanes] * scale).astype(bf16)
        return carry

    lax.fori_loop(0, NW // 128, to_modes, 0)

    def to_owner(step, carry):
        owner = lax.rem(g + step, GROUPS)
        at = pl.ds(pl.multiple_of(owner * 96, 32), 96)
        value = jnp.dot(rows[at, :], damped[...], preferred_element_type=f32).astype(bf16)
        stacked = jnp.concatenate([value[:, t * 128 : (t + 1) * 128] for t in range(TRACERS)], 0)
        wide = jnp.dot(spread[...], stacked, preferred_element_type=f32)
        wide = wide.reshape(BANDS, 16, 128).astype(bf16)
        send2[pl.ds(owner * BANDS, BANDS)] = wide[:, :ROWS]
        for a, c in PAIRS:
            for dz in ZSTEPS:
                to = peer(step, a, dz, c)

                def push():
                    remote(
                        send2.at[owner * BANDS + to[1]],
                        recv2.at[g, half, z, core],
                        2,
                        (owner, to[1]),
                    ).start()

                if a or c or dz:
                    push()
                else:
                    pl.when(step != 0)(push)
        return carry

    lax.fori_loop(0, GROUPS, to_owner, 0)
    own2 = pltpu.make_async_copy(
        send2.at[g * BANDS + b], recv2.at[g, half, z, core], local_sem.at[2]
    )
    own2.start()
    own2.wait()
    wait_bytes(send2.at[pl.ds(0, GROUPS * BANDS - 1)], recv_sem.at[2])

    for block in range(BLOCKS):
        value = recv2[:, :, block, :, :, :].astype(f32).reshape(MEMBERS, ROWS, 128)
        padded[:, :ROWS, block * 128 : (block + 1) * 128] = value

    def permute(i, carry):
        lanes = pl.ds(pl.multiple_of(i * 256, 256), 256)
        value = padded[:, :, lanes].reshape(MEMBERS * 16, 256).astype(bf16)
        coefficients[:, lanes] = jnp.dot(
            gather[...], value, preferred_element_type=f32
        ).astype(bf16)
        return carry

    lax.fori_loop(0, 4, permute, 0)

    obs = cells.shape[-1]

    def background_step(c, carry):
        smooth = jnp.dot(coefficients[...], inverse[c], preferred_element_type=f32)
        smooth = smooth.reshape(TRACERS, PLAT, MEMBERS, PLON)
        for j in range(PLAT):
            for h in range(PLON // 128):
                lanes = pl.ds(pl.multiple_of(c * PLON + h * 128, 128), 128)
                tracers = [smooth[t, j, :, h * 128 : (h + 1) * 128] for t in range(TRACERS)]
                rates = []
                for r in range(REACTIONS):
                    line = field_rows[r, j : j + 1, lanes]
                    rates.append(fac_wide[c, r] * line)
                leave, gone = [], []
                for s in range(TRACERS):
                    outflow = rates[3 * s] + rates[3 * s + 1] + rates[3 * s + 2]
                    leave.append(1.0 / (1.0 + outflow))
                    gone.append(leave[s] * tracers[s])
                for t in range(TRACERS):
                    value = gone[t]
                    for s in range(TRACERS):
                        if s != t:
                            value = value + rates[3 * s + (t if t < s else t - 1)] * gone[s]
                    row = (t * PLAT + j) * MEMBERS
                    background[c, row : row + MEMBERS, h * 128 : (h + 1) * 128] = value.astype(
                        bf16
                    )
        cell = cells[g, pl.ds(c, 1), :]
        column = jnp.bitwise_and(cell, PLON - 1)
        row = lax.shift_right_logical(cell, 8)
        picker = jnp.where(
            lax.broadcasted_iota(jnp.int32, (PLON, obs), 0) == column, 1.0, 0.0
        ).astype(bf16)
        seen = jnp.dot(background[c], picker, preferred_element_type=f32)
        predicted = jnp.zeros((MEMBERS, obs), f32)
        for k in range(ROWS):
            predicted = predicted + jnp.where(
                row == k, seen[k * MEMBERS : (k + 1) * MEMBERS], 0.0
            )
        seen_mean = jnp.mean(predicted, axis=0, keepdims=True)
        spread_of = predicted - seen_mean
        weight = spread_of * (1.0 / variance[g, pl.ds(c, 1), :])
        innovation = measured[g, pl.ds(c, 1), :] - seen_mean
        at = pl.ds(pl.multiple_of(c * MEMBERS, MEMBERS), MEMBERS)
        weighted[at, :] = weight
        spread_seen[at, :] = spread_of
        projected[at, :] = jnp.broadcast_to(
            jnp.sum(weight * innovation, axis=1, keepdims=True), (MEMBERS, 128)
        )
        return carry

    lax.fori_loop(0, PATCHES, background_step, 0)

    size = PATCHES * MEMBERS
    block_row = lax.broadcasted_iota(jnp.int32, (size, size), 0)
    block_col = lax.broadcasted_iota(jnp.int32, (size, size), 1)
    same = block_row // MEMBERS == block_col // MEMBERS
    identity = jnp.where(block_row == block_col, 1.0, 0.0)

    def exact(left, right):
        return jnp.dot(left, right, precision=HI, preferred_element_type=f32)

    outer = lax.dot_general(
        weighted[...],
        spread_seen[...],
        (((1,), (1,)), ((), ())),
        precision=HI,
        preferred_element_type=f32,
    )
    outer = jnp.where(same, outer, 0.0)
    square = jnp.sum(outer * outer, axis=1, keepdims=True).reshape(PATCHES, MEMBERS, 1)
    square = jnp.broadcast_to(jnp.sum(square, axis=1, keepdims=True), (PATCHES, MEMBERS, 1))
    scale = (MEMBERS - 1.0) + jnp.sqrt(square.reshape(size, 1))
    current = ((MEMBERS - 1.0) * identity + outer) / scale
    root = 1.5 * identity - 0.5 * current
    current = exact(current, root)
    for sweep in range(1, SWEEPS):
        middle = 1.5 * identity - 0.5 * exact(root, current)
        if sweep < SWEEPS - 1:
            current = exact(current, middle)
        root = exact(middle, root)
    mean_weight = exact(root, exact(root, projected[...])) / scale
    full = jnp.where(same, jnp.sqrt((MEMBERS - 1.0) / scale) * root, 0.0)
    fold = jnp.where(
        lax.rem(lax.broadcasted_iota(jnp.int32, (size, MEMBERS), 0), MEMBERS)
        == lax.broadcasted_iota(jnp.int32, (size, MEMBERS), 1),
        1.0,
        0.0,
    )
    transform[...] = exact(full, fold) + mean_weight[:, :MEMBERS]

    def apply(matrix, values, precision=None):
        return lax.dot_general(
            matrix,
            values,
            (((0,), (0,)), ((), ())),
            precision=precision,
            preferred_element_type=f32,
        )

    def analysis_step(c, carry):
        matrix = transform[pl.ds(pl.multiple_of(c * MEMBERS, MEMBERS), MEMBERS), :]
        pieces = []
        for k in range(ROWS):
            value = background[c, k * MEMBERS : (k + 1) * MEMBERS, :].astype(f32)
            center = jnp.mean(value, axis=0, keepdims=True)
            pieces.append((center + apply(matrix, value - center)).astype(bf16))
        analysed = jnp.concatenate(pieces, axis=0)
        sent = jnp.dot(home[...], analysed, preferred_element_type=f32).astype(bf16)
        send3[c] = sent.reshape(GROUPS, LOCAL * ROWS, PLON)
        lanes = pl.ds(pl.multiple_of(c * PLON, PLON), PLON)
        for step in range(1, GROUPS):
            to = lax.rem(g + step, GROUPS)
            remote(send3.at[c, to], out_hbm.at[g, :, lanes], 3, (to, b)).start()
        pltpu.make_async_copy(
            send3.at[c, g], out_hbm.at[g, :, lanes], local_sem.at[3]
        ).start()
        lane = lax.broadcasted_iota(jnp.int32, (MEMBERS, 128), 1)
        mine = jnp.logical_and(lane >= c * REACTIONS, lane < (c + 1) * REACTIONS)
        return carry + jnp.where(mine, apply(matrix, log_spread, HI), 0.0)

    change = lax.fori_loop(0, PATCHES, analysis_step, jnp.zeros((MEMBERS, 128), f32))
    mult = jnp.exp(log_mean + change).astype(bf16)
    back_row = lax.broadcasted_iota(jnp.int32, (GROUPS * 8, MEMBERS), 0)
    back_col = lax.broadcasted_iota(jnp.int32, (GROUPS * 8, MEMBERS), 1)
    place = (back_col // LOCAL) * 8 + lax.rem(back_col, LOCAL)
    put = jnp.where(back_row == place, 1.0, 0.0).astype(bf16)
    mult_send[...] = jnp.dot(put, mult, preferred_element_type=f32).reshape(GROUPS, 8, 128)
    for step in range(1, GROUPS):
        to = lax.rem(g + step, GROUPS)
        remote(mult_send.at[to], mult_in.at[g], 4, (to, b)).start()
    own_mult = pltpu.make_async_copy(mult_send.at[g], mult_in.at[g], local_sem.at[4])
    own_mult.start()

    own_mult.wait()
    wait_bytes(mult_in.at[pl.ds(0, GROUPS - 1)], recv_sem.at[4])
    mult_out[...] = mult_in[...]
    wait_bytes(send3.at[:, 0], local_sem.at[3])
    wait_bytes(send3.at[:, pl.ds(0, GROUPS - 1)], recv_sem.at[3])
    wait_bytes(send1.at[pl.ds(0, BLOCKS - 1)], send_sem.at[0])
    wait_bytes(send1.at[0, pl.ds(0, LOCAL - 1)], send_sem.at[0])
    wait_bytes(send2.at[pl.ds(0, GROUPS * BANDS - 1)], send_sem.at[2])
    wait_bytes(send3.at[:, pl.ds(0, GROUPS - 1)], send_sem.at[3])
    wait_bytes(mult_send.at[pl.ds(0, GROUPS - 1)], send_sem.at[4])


def on_device(x, field, kinetic, cells, measured, variance):
    forward, inverse, modes, rows, gain, spread, gather, home = tables()
    fac = kinetic.transpose(2, 0, 3, 1).reshape(GROUPS, LOCAL, PATCHES * REACTIONS).astype(f32)
    fac = jnp.pad(
        fac, ((0, 0), (0, 8 - LOCAL), (0, 128 - PATCHES * REACTIONS)), constant_values=1.0
    )
    anywhere = pl.BlockSpec(memory_space=pl.ANY)
    vmem = pl.BlockSpec(memory_space=pltpu.VMEM)
    size = PATCHES * MEMBERS
    scratch = [
        pltpu.VMEM((LOCAL, TRACERS, BAND, NLON), f32),
        pltpu.VMEM((LOCAL * TRACERS * BAND, NLON), bf16),
        pltpu.VMEM((4, NLON, 256), bf16),
        pltpu.VMEM((PATCHES, 2 * NW, PLON), bf16),
        pltpu.VMEM((NW, NLAT), bf16),
        pltpu.VMEM((NLAT, NW), bf16),
        pltpu.VMEM((NW, 128), f32),
        pltpu.VMEM(spread.shape, bf16),
        pltpu.VMEM(gather.shape, bf16),
        pltpu.VMEM(home.shape, bf16),
        pltpu.VMEM((REACTIONS, BAND, NLON), bf16),
        pltpu.VMEM((REACTIONS, 8, NLON), f32),
        pltpu.VMEM((BLOCKS, LOCAL, TRACERS * BAND, 128), bf16),
        pltpu.VMEM((BANDS, TRACERS * BAND, 128), bf16),
        pltpu.VMEM((NLAT, TRACERS * 128), f32),
        pltpu.VMEM((NLAT, TRACERS * 128), bf16),
        pltpu.VMEM((NW, TRACERS * 128), bf16),
        pltpu.VMEM((GROUPS * BANDS, ROWS, 128), bf16),
        pltpu.VMEM((GROUPS, 2, BLOCKS, 2, ROWS, 128), bf16),
        pltpu.VMEM((MEMBERS, 16, BLOCKS * 128), f32),
        pltpu.VMEM((ROWS * MEMBERS, 2 * NW), bf16),
        pltpu.VMEM((GROUPS, 8, 128), f32),
        pltpu.VMEM((PATCHES, REACTIONS, MEMBERS, 128), f32),
        pltpu.VMEM((PATCHES, ROWS * MEMBERS, PLON), bf16),
        pltpu.VMEM((size, 128), f32),
        pltpu.VMEM((size, 128), f32),
        pltpu.VMEM((size, 128), f32),
        pltpu.VMEM((size, MEMBERS), f32),
        pltpu.VMEM((PATCHES, GROUPS, LOCAL * ROWS, PLON), bf16),
        pltpu.VMEM((GROUPS, 8, 128), f32),
        pltpu.VMEM((GROUPS, 8, 128), f32),
        pltpu.SemaphoreType.DMA((13,)),
        pltpu.SemaphoreType.DMA((5,)),
        pltpu.SemaphoreType.DMA((5,)),
        pltpu.SemaphoreType.DMA((5,)),
    ]
    out, mult = pl.pallas_call(
        kernel,
        out_shape=(
            jax.ShapeDtypeStruct((GROUPS, LOCAL * ROWS, NLON), bf16),
            jax.ShapeDtypeStruct((GROUPS, 8, 128), f32),
        ),
        in_specs=[anywhere, vmem, vmem, vmem, vmem, anywhere] + [anywhere] * 8,
        out_specs=(anywhere, vmem),
        scratch_shapes=scratch,
        compiler_params=pltpu.CompilerParams(
            collective_id=0, has_side_effects=True, vmem_limit_bytes=60 << 20
        ),
        name="assimilate",
    )(x, fac, cells, measured, variance, field, forward, inverse, modes, rows, gain, spread, gather, home)
    analysis = (
        out.reshape(GROUPS, LOCAL, TRACERS, PLAT, NLON)
        .transpose(1, 2, 0, 3, 4)
        .reshape(LOCAL, TRACERS, BAND, NLON)
    )
    mult = (
        mult[:, :LOCAL, : PATCHES * REACTIONS]
        .reshape(GROUPS, LOCAL, PATCHES, REACTIONS)
        .transpose(1, 3, 0, 2)
        .astype(bf16)
    )
    return analysis, mult


def solution(mesh):
    return jax.shard_map(
        on_device,
        mesh=mesh,
        in_specs=(
            P("mem", None, "grid", None),
            P(None, "grid", None),
            P("mem", None, "grid", None),
            P("grid", None, None),
            P("grid", None, None),
            P("grid", None, None),
        ),
        out_specs=(P("mem", None, "grid", None), P("mem", None, "grid", None)),
        check_vma=False,
    )
```

profile of v0, /device:TPU:1, one launch (start us, length us, event | category | flops | bytes accessed | tf_op | source)
XLA Modules:
  0.0 100.6 jit_solution(9024451854029395597)
XLA Ops:
  0.6 1.4 %copy.24.cells = s32[8,6,128]{2,1,0:T(8,128)} copy(s32[8,6,128]{2,0,1:T(8,128)} %param.17) | data formatting | bytes 49152 | tf_op args[3]
  2.0 1.3 %copy.25.measured = f32[8,6,128]{2,1,0:T(8,128)} copy(f32[8,6,128]{2,0,1:T(8,128)} %param.18) | data formatting | bytes 49152 | tf_op args[4]
  3.3 1.4 %copy.26.variance = f32[8,6,128]{2,1,0:T(8,128)} copy(f32[8,6,128]{2,0,1:T(8,128)} %param.19) | data formatting | bytes 49152 | tf_op args[5]
  4.7 0.8 copy.32
  5.5 0.1 reshape.17
  5.6 0.6 pad_convert_fusion.fac
  6.2 89.2 %assimilate.1 = (bf16[8,48,1536]{2,1,0:T(8,128)(2,1)}, f32[8,8,128]{2,1,0:T(8,128)}) custom-call(f32[4,4,24,1536]{3,2,1,0:T(8,128)} %x_hbm.1, f32[8,8,128]{2,1,0:T(8,128)} %pad_convert_fusion.fac, s32[8,6,128]{2,1,0:T(8,128)} %copy.24.cells, f32[8,6,128]{2,1,0:T(8,128)} %copy.25.measured, f32[8,6,128]{2,1,0:T(8,128)} %copy.26.variance, ...), custom_call_target="tpu_custom_call" | custom-call | tf_op jit(solution)/shard_map/assimilate/pallas_call | solution.py:544
  95.4 1.9 %copy.27 = bf16[8,48,1536]{2,0,1:T(8,128)(2,1)S(1)} copy(bf16[8,48,1536]{2,1,0:T(8,128)(2,1)} %get-tuple-element.4) | data formatting | bytes 2359296 | tf_op jit(solution)/shard_map/assimilate/pallas_call | solution.py:544
  97.3 0.6 copy.28
  97.9 1.2 %copy.30 = bf16[4,4,24,1536]{3,2,1,0:T(8,128)(2,1)} copy(bf16[4,4,24,1536]{3,1,2,0:T(4,128)(2,1)S(1)} %bitcast.9) | data formatting | bytes 2359296
  99.2 0.8 slice.7
  99.9 0.1 convert_element_type.16
  100.0 0.6 copy.31
  (1 shorter events, 0.0 us)
where the time goes:
time: 101 us
  Pallas kernels  89.2 us (88%)
  local copies, waits for them, and re-layouts  10.2 us (10%)
    pallas_call x1, Pallas kernels, on_device(): pl.pallas_call(kernel, out_shape=(jax.ShapeDtypeStruct((GROUPS, LOCAL * R...  89.2 us
    unnamed x5, local copies, waits for them, and re-layouts  5.91 us

commit v1 on v0

--- a/solution.py
+++ b/solution.py
@@ -25,13 +25,15 @@
 BANDS = 32
 LOCAL = 4
 BLOCKS = 8
+TOGETHER = 3
 BAND = NLAT // BANDS
 PATCHES = NLON // PLON
 ROWS = TRACERS * PLAT
 MESH = pl.DeviceIdType.MESH
 HI = lax.Precision.HIGHEST
+
+PAIRS = ((1, 1), (0, 1), (1, 0), (0, 0))
 ZSTEPS = (4, 3, 5, 2, 6, 1, 7, 0)
-PAIRS = ((1, 1), (0, 1), (1, 0), (0, 0))
 
 f32 = jnp.float32
 bf16 = jnp.bfloat16
@@ -90,28 +92,41 @@
             for a in range(ROWS):
                 home[g, e, a, a, g, e] = 1.0
     home = home.reshape(MEMBERS * ROWS, ROWS * MEMBERS)
+    index = np.arange(LOCAL * PATCHES * GROUPS)
+    e, c, g = np.unravel_index(index, (LOCAL, PATCHES, GROUPS))
+    by_group = np.zeros((index.size, index.size), np.float32)
+    by_group[(g * LOCAL + e) * PATCHES + c, index] = 1.0
+    g, e, c = np.unravel_index(index, (GROUPS, LOCAL, PATCHES))
+    by_patch = np.zeros((index.size, index.size), np.float32)
+    by_patch[(c * GROUPS + g) * LOCAL + e, index] = 1.0
+    small = np.stack([by_group, by_patch, by_patch.T, by_group.T])
+    index = np.arange(GROUPS * LOCAL * ROWS)
+    g, et, j = np.unravel_index(index, (GROUPS, LOCAL * TRACERS, PLAT))
+    final = np.zeros((index.size, index.size), np.float32)
+    final[(et * GROUPS + g) * PLAT + j, index] = 1.0
     b = lambda v: np.asarray(v, np.float32).astype(ml_dtypes.bfloat16)
-    return b(forward), b(inverse), b(to_modes), b(to_rows), gain, b(spread), b(gather), b(home)
+    return (
+        (b(forward), b(inverse), b(to_modes), b(to_rows), gain)
+        + (b(spread), b(gather), b(home), b(small)),
+        b(final),
+    )
 
 
 def split_grid(b):
     return b // 16, lax.rem(b // 2, 8), lax.rem(b, 2)
 
 
-def peer(group_step, a, dz, c):
-    g, b = lax.axis_index("mem"), lax.axis_index("grid")
-    half, z, core = split_grid(b)
-    band = lax.rem(half + a, 2) * 16 + lax.rem(z + dz, 8) * 2 + lax.rem(core + c, 2)
-    return lax.rem(g + group_step, GROUPS), band
+def wrap(value, size):
+    return jnp.where(value >= size, value - size, value)
 
 
 def kernel(
     x_hbm,
-    fac,
-    cells,
-    measured,
-    variance,
     field_hbm,
+    fac_hbm,
+    cells_hbm,
+    measured_hbm,
+    variance_hbm,
     forward_hbm,
     inverse_hbm,
     modes_hbm,
@@ -120,6 +135,7 @@
     spread_hbm,
     gather_hbm,
     home_hbm,
+    small_hbm,
     out_hbm,
     mult_out,
     x,
@@ -132,6 +148,11 @@
     spread,
     gather,
     home,
+    small,
+    fac_raw,
+    cells,
+    measured,
+    variance,
     field,
     field_rows,
     send1,
@@ -143,8 +164,12 @@
     recv2,
     padded,
     coefficients,
+    fac,
     fac_in,
     fac_wide,
+    log_mean,
+    log_spread,
+    log_new,
     background,
     weighted,
     spread_seen,
@@ -157,6 +182,7 @@
     local_sem,
     send_sem,
     recv_sem,
+    ready,
 ):
     g, b = lax.axis_index("mem"), lax.axis_index("grid")
     half, z, core = split_grid(b)
@@ -167,6 +193,9 @@
 
     load_x = load(x_hbm, x, 0)
     load_x.start()
+    load_fac = [load(fac_hbm, fac_raw, 13), load(small_hbm, small, 14)]
+    for one in load_fac:
+        one.start()
     load_forward = [load(forward_hbm.at[i], forward.at[i], 1 + i) for i in range(4)]
     for one in load_forward:
         one.start()
@@ -180,28 +209,26 @@
         load(inverse_hbm, inverse, 10),
         load(gather_hbm, gather, 11),
         load(home_hbm, home, 12),
+        load(cells_hbm, cells, 15),
+        load(measured_hbm, measured, 16),
+        load(variance_hbm, variance, 17),
     ]
     for one in later:
         one.start()
 
     barrier = pltpu.get_barrier_semaphore()
 
-    def greet(step, carry):
-        for a, c in PAIRS:
-            for dz in ZSTEPS:
-
-                def signal():
-                    pl.semaphore_signal(
-                        barrier, inc=1, device_id=peer(step, a, dz, c), device_id_type=MESH
-                    )
-
-                if a or c or dz:
-                    signal()
-                else:
-                    pl.when(step != 0)(signal)
-        return carry
-
-    lax.fori_loop(0, GROUPS, greet, 0)
+    groups = [wrap(g + step, GROUPS) for step in range(1, GROUPS)]
+    bands = [
+        wrap(half + a, 2) * 16 + wrap(z + dz, BLOCKS) * 2 + wrap(core + c, 2)
+        for a, c in PAIRS
+        for dz in ZSTEPS
+        if a or c or dz
+    ]
+    for to in groups:
+        pl.semaphore_signal(barrier, inc=1, device_id=(to, b), device_id_type=MESH)
+    for to in bands:
+        pl.semaphore_signal(barrier, inc=1, device_id=(g, to), device_id_type=MESH)
 
     load_x.wait()
     xb[...] = x[...].reshape(LOCAL * TRACERS * BAND, NLON).astype(bf16)
@@ -216,7 +243,9 @@
         return carry
 
     lax.fori_loop(0, 4, forward_step, 0)
-    pl.semaphore_wait(barrier, GROUPS * BANDS - 1)
+    pl.semaphore_wait(barrier, GROUPS + BANDS - 2)
+    for to in groups:
+        pl.semaphore_signal(ready, inc=1, device_id=(to, b), device_id_type=MESH)
 
     def remote(src, dst, i, to):
         return pltpu.make_async_remote_copy(
@@ -231,16 +260,19 @@
     def wait_bytes(ref, sem):
         pltpu.make_async_copy(ref, ref, sem).wait()
 
-    for a, c in PAIRS:
-        for dz in ZSTEPS:
-            if a or c or dz:
-                _, band = peer(0, a, dz, c)
-                h2, z2, c2 = split_grid(band)
-                remote(send1.at[z2, h2 * 2 + c2], recv1.at[b], 0, (g, band)).start()
+    for band in bands:
+        h2, z2, c2 = split_grid(band)
+        remote(send1.at[z2, h2 * 2 + c2], recv1.at[b], 0, (g, band)).start()
     own1 = pltpu.make_async_copy(send1.at[z, member], recv1.at[b], local_sem.at[0])
     own1.start()
-    for step in range(1, GROUPS):
-        to = lax.rem(g + step, GROUPS)
+    pairs = LOCAL * PATCHES
+    for one in load_fac:
+        one.wait()
+    raw = fac_raw[...].astype(f32).reshape(pairs * GROUPS, REACTIONS).astype(bf16)
+    fac[...] = jnp.ones(fac.shape, f32)
+    raw = jnp.dot(small[0], raw, preferred_element_type=f32)
+    fac[:, :, :REACTIONS] = raw.reshape(GROUPS, pairs, REACTIONS)
+    for to in groups:
         remote(fac.at[to], fac_in.at[g], 1, (to, b)).start()
     own_fac = pltpu.make_async_copy(fac.at[g], fac_in.at[g], local_sem.at[1])
     own_fac.start()
@@ -261,21 +293,20 @@
     own_fac.wait()
     wait_bytes(fac_in.at[pl.ds(0, GROUPS - 1)], recv_sem.at[1])
     wait_bytes(fac.at[pl.ds(0, GROUPS - 1)], send_sem.at[1])
-    row_of = lax.broadcasted_iota(jnp.int32, (MEMBERS, GROUPS * 8), 0)
-    col_of = lax.broadcasted_iota(jnp.int32, (MEMBERS, GROUPS * 8), 1)
-    pick = jnp.where(col_of == (row_of // LOCAL) * 8 + lax.rem(row_of, LOCAL), 1.0, 0.0)
     factors = jnp.dot(
-        pick.astype(bf16),
-        fac_in[...].reshape(GROUPS * 8, 128).astype(bf16),
+        small[1],
+        fac_in[...].reshape(GROUPS * pairs, 128).astype(bf16),
         preferred_element_type=f32,
     )
     for c in range(PATCHES):
         for r in range(REACTIONS):
-            lane = c * REACTIONS + r
-            fac_wide[c, r] = jnp.broadcast_to(factors[:, lane : lane + 1], (MEMBERS, 128))
-    log_rate = jnp.log(factors)
-    log_mean = jnp.mean(log_rate, axis=0, keepdims=True)
-    log_spread = log_rate - log_mean
+            column = factors[c * MEMBERS : (c + 1) * MEMBERS, r : r + 1]
+            fac_wide[c, r] = jnp.broadcast_to(column, (MEMBERS, 128))
+    log_rate = jnp.log(factors).reshape(PATCHES, MEMBERS, 128)
+    log_mean[...] = jnp.broadcast_to(
+        jnp.mean(log_rate, axis=1, keepdims=True), (PATCHES, MEMBERS, 128)
+    )
+    log_spread[...] = log_rate - log_mean[...]
 
     own1.wait()
     wait_bytes(recv1.at[pl.ds(0, BANDS - 1)], recv_sem.at[0])
@@ -302,31 +333,30 @@
     lax.fori_loop(0, NW // 128, to_modes, 0)
 
     def to_owner(step, carry):
-        owner = lax.rem(g + step, GROUPS)
+        owner = wrap(g + step, GROUPS)
         at = pl.ds(pl.multiple_of(owner * 96, 32), 96)
         value = jnp.dot(rows[at, :], damped[...], preferred_element_type=f32).astype(bf16)
         stacked = jnp.concatenate([value[:, t * 128 : (t + 1) * 128] for t in range(TRACERS)], 0)
         wide = jnp.dot(spread[...], stacked, preferred_element_type=f32)
         wide = wide.reshape(BANDS, 16, 128).astype(bf16)
         send2[pl.ds(owner * BANDS, BANDS)] = wide[:, :ROWS]
-        for a, c in PAIRS:
-            for dz in ZSTEPS:
-                to = peer(step, a, dz, c)
-
-                def push():
-                    remote(
-                        send2.at[owner * BANDS + to[1]],
-                        recv2.at[g, half, z, core],
-                        2,
-                        (owner, to[1]),
-                    ).start()
-
-                if a or c or dz:
-                    push()
-                else:
-                    pl.when(step != 0)(push)
+        for band in bands:
+            remote(
+                send2.at[owner * BANDS + band],
+                recv2.at[g, half, z, core],
+                2,
+                (owner, band),
+            ).start()
+
+        @pl.when(step != 0)
+        def _():
+            remote(
+                send2.at[owner * BANDS + b], recv2.at[g, half, z, core], 2, (owner, b)
+            ).start()
+
         return carry
 
+    pl.semaphore_wait(ready, GROUPS - 1)
     lax.fori_loop(0, GROUPS, to_owner, 0)
     own2 = pltpu.make_async_copy(
         send2.at[g * BANDS + b], recv2.at[g, half, z, core], local_sem.at[2]
@@ -351,7 +381,8 @@
 
     obs = cells.shape[-1]
 
-    def background_step(c, carry):
+    def background_step(i, first):
+        c = first + i
         smooth = jnp.dot(coefficients[...], inverse[c], preferred_element_type=f32)
         smooth = smooth.reshape(TRACERS, PLAT, MEMBERS, PLON)
         for j in range(PLAT):
@@ -376,7 +407,7 @@
                     background[c, row : row + MEMBERS, h * 128 : (h + 1) * 128] = value.astype(
                         bf16
                     )
-        cell = cells[g, pl.ds(c, 1), :]
+        cell = cells[c, pl.ds(g, 1), :]
         column = jnp.bitwise_and(cell, PLON - 1)
         row = lax.shift_right_logical(cell, 8)
         picker = jnp.where(
@@ -390,55 +421,60 @@
             )
         seen_mean = jnp.mean(predicted, axis=0, keepdims=True)
         spread_of = predicted - seen_mean
-        weight = spread_of * (1.0 / variance[g, pl.ds(c, 1), :])
-        innovation = measured[g, pl.ds(c, 1), :] - seen_mean
-        at = pl.ds(pl.multiple_of(c * MEMBERS, MEMBERS), MEMBERS)
+        weight = spread_of * (1.0 / variance[c, pl.ds(g, 1), :])
+        innovation = measured[c, pl.ds(g, 1), :] - seen_mean
+        at = pl.ds(pl.multiple_of(i * MEMBERS, MEMBERS), MEMBERS)
         weighted[at, :] = weight
         spread_seen[at, :] = spread_of
         projected[at, :] = jnp.broadcast_to(
             jnp.sum(weight * innovation, axis=1, keepdims=True), (MEMBERS, 128)
         )
-        return carry
-
-    lax.fori_loop(0, PATCHES, background_step, 0)
-
-    size = PATCHES * MEMBERS
+        return first
+
+    size = TOGETHER * MEMBERS
     block_row = lax.broadcasted_iota(jnp.int32, (size, size), 0)
     block_col = lax.broadcasted_iota(jnp.int32, (size, size), 1)
     same = block_row // MEMBERS == block_col // MEMBERS
     identity = jnp.where(block_row == block_col, 1.0, 0.0)
 
+    def halves(value):
+        high = value.astype(bf16)
+        return high, (value - high.astype(f32)).astype(bf16)
+
     def exact(left, right):
-        return jnp.dot(left, right, precision=HI, preferred_element_type=f32)
-
-    outer = lax.dot_general(
-        weighted[...],
-        spread_seen[...],
-        (((1,), (1,)), ((), ())),
-        precision=HI,
-        preferred_element_type=f32,
-    )
-    outer = jnp.where(same, outer, 0.0)
-    square = jnp.sum(outer * outer, axis=1, keepdims=True).reshape(PATCHES, MEMBERS, 1)
-    square = jnp.broadcast_to(jnp.sum(square, axis=1, keepdims=True), (PATCHES, MEMBERS, 1))
-    scale = (MEMBERS - 1.0) + jnp.sqrt(square.reshape(size, 1))
-    current = ((MEMBERS - 1.0) * identity + outer) / scale
-    root = 1.5 * identity - 0.5 * current
-    current = exact(current, root)
-    for sweep in range(1, SWEEPS):
-        middle = 1.5 * identity - 0.5 * exact(root, current)
-        if sweep < SWEEPS - 1:
-            current = exact(current, middle)
-        root = exact(middle, root)
-    mean_weight = exact(root, exact(root, projected[...])) / scale
-    full = jnp.where(same, jnp.sqrt((MEMBERS - 1.0) / scale) * root, 0.0)
-    fold = jnp.where(
-        lax.rem(lax.broadcasted_iota(jnp.int32, (size, MEMBERS), 0), MEMBERS)
-        == lax.broadcasted_iota(jnp.int32, (size, MEMBERS), 1),
-        1.0,
-        0.0,
-    )
-    transform[...] = exact(full, fold) + mean_weight[:, :MEMBERS]
+        (a, b), (c, d) = halves(left), halves(right)
+        dot = functools.partial(jnp.dot, preferred_element_type=f32)
+        return dot(a, c) + (dot(a, d) + dot(b, c))
+
+    def solve():
+        outer = lax.dot_general(
+            weighted[...],
+            spread_seen[...],
+            (((1,), (1,)), ((), ())),
+            precision=HI,
+            preferred_element_type=f32,
+        )
+        outer = jnp.where(same, outer, 0.0)
+        square = jnp.sum(outer * outer, axis=1, keepdims=True).reshape(TOGETHER, MEMBERS, 1)
+        square = jnp.broadcast_to(jnp.sum(square, axis=1, keepdims=True), (TOGETHER, MEMBERS, 1))
+        scale = (MEMBERS - 1.0) + jnp.sqrt(square.reshape(size, 1))
+        current = ((MEMBERS - 1.0) * identity + outer) / scale
+        root = 1.5 * identity - 0.5 * current
+        current = exact(current, root)
+        for sweep in range(1, SWEEPS):
+            middle = 1.5 * identity - 0.5 * exact(root, current)
+            if sweep < SWEEPS - 1:
+                current = exact(current, middle)
+            root = exact(middle, root)
+        mean_weight = exact(root, exact(root, projected[...])) / scale
+        full = jnp.where(same, jnp.sqrt((MEMBERS - 1.0) / scale) * root, 0.0)
+        fold = jnp.where(
+            lax.rem(lax.broadcasted_iota(jnp.int32, (size, MEMBERS), 0), MEMBERS)
+            == lax.broadcasted_iota(jnp.int32, (size, MEMBERS), 1),
+            1.0,
+            0.0,
+        )
+        transform[...] = exact(full, fold) + mean_weight[:, :MEMBERS]
 
     def apply(matrix, values, precision=None):
         return lax.dot_general(
@@ -449,8 +485,9 @@
             preferred_element_type=f32,
         )
 
-    def analysis_step(c, carry):
-        matrix = transform[pl.ds(pl.multiple_of(c * MEMBERS, MEMBERS), MEMBERS), :]
+    def analysis_step(i, first):
+        c = first + i
+        matrix = transform[pl.ds(pl.multiple_of(i * MEMBERS, MEMBERS), MEMBERS), :]
         pieces = []
         for k in range(ROWS):
             value = background[c, k * MEMBERS : (k + 1) * MEMBERS, :].astype(f32)
@@ -460,32 +497,35 @@
         sent = jnp.dot(home[...], analysed, preferred_element_type=f32).astype(bf16)
         send3[c] = sent.reshape(GROUPS, LOCAL * ROWS, PLON)
         lanes = pl.ds(pl.multiple_of(c * PLON, PLON), PLON)
-        for step in range(1, GROUPS):
-            to = lax.rem(g + step, GROUPS)
+        for to in groups:
             remote(send3.at[c, to], out_hbm.at[g, :, lanes], 3, (to, b)).start()
         pltpu.make_async_copy(
             send3.at[c, g], out_hbm.at[g, :, lanes], local_sem.at[3]
         ).start()
-        lane = lax.broadcasted_iota(jnp.int32, (MEMBERS, 128), 1)
-        mine = jnp.logical_and(lane >= c * REACTIONS, lane < (c + 1) * REACTIONS)
-        return carry + jnp.where(mine, apply(matrix, log_spread, HI), 0.0)
-
-    change = lax.fori_loop(0, PATCHES, analysis_step, jnp.zeros((MEMBERS, 128), f32))
-    mult = jnp.exp(log_mean + change).astype(bf16)
-    back_row = lax.broadcasted_iota(jnp.int32, (GROUPS * 8, MEMBERS), 0)
-    back_col = lax.broadcasted_iota(jnp.int32, (GROUPS * 8, MEMBERS), 1)
-    place = (back_col // LOCAL) * 8 + lax.rem(back_col, LOCAL)
-    put = jnp.where(back_row == place, 1.0, 0.0).astype(bf16)
-    mult_send[...] = jnp.dot(put, mult, preferred_element_type=f32).reshape(GROUPS, 8, 128)
-    for step in range(1, GROUPS):
-        to = lax.rem(g + step, GROUPS)
+        log_new[c] = jnp.exp(log_mean[c] + apply(matrix, log_spread[c], HI))
+        return first
+
+    def group_step(i, carry):
+        first = i * TOGETHER
+        lax.fori_loop(0, TOGETHER, background_step, first)
+        solve()
+        lax.fori_loop(0, TOGETHER, analysis_step, first)
+        return carry
+
+    lax.fori_loop(0, PATCHES // TOGETHER, group_step, 0)
+    mult = log_new[...].reshape(PATCHES * MEMBERS, 128).astype(bf16)
+    mult = jnp.dot(small[2], mult, preferred_element_type=f32)
+    mult_send[...] = mult.reshape(GROUPS, pairs, 128)
+    for to in groups:
         remote(mult_send.at[to], mult_in.at[g], 4, (to, b)).start()
     own_mult = pltpu.make_async_copy(mult_send.at[g], mult_in.at[g], local_sem.at[4])
     own_mult.start()
 
     own_mult.wait()
     wait_bytes(mult_in.at[pl.ds(0, GROUPS - 1)], recv_sem.at[4])
-    mult_out[...] = mult_in[...]
+    mult = mult_in[...].reshape(GROUPS * pairs, 128).astype(bf16)
+    mult = jnp.dot(small[3], mult, preferred_element_type=f32)
+    mult_out[...] = mult.reshape(LOCAL, PATCHES, GROUPS, 128)[..., :REACTIONS].astype(bf16)
     wait_bytes(send3.at[:, 0], local_sem.at[3])
     wait_bytes(send3.at[:, pl.ds(0, GROUPS - 1)], recv_sem.at[3])
     wait_bytes(send1.at[pl.ds(0, BLOCKS - 1)], send_sem.at[0])
@@ -496,14 +536,12 @@
 
 
 def on_device(x, field, kinetic, cells, measured, variance):
-    forward, inverse, modes, rows, gain, spread, gather, home = tables()
-    fac = kinetic.transpose(2, 0, 3, 1).reshape(GROUPS, LOCAL, PATCHES * REACTIONS).astype(f32)
-    fac = jnp.pad(
-        fac, ((0, 0), (0, 8 - LOCAL), (0, 128 - PATCHES * REACTIONS)), constant_values=1.0
-    )
+    constants, final = tables()
     anywhere = pl.BlockSpec(memory_space=pl.ANY)
     vmem = pl.BlockSpec(memory_space=pltpu.VMEM)
-    size = PATCHES * MEMBERS
+    size = TOGETHER * MEMBERS
+    pairs = LOCAL * PATCHES
+    obs = cells.shape[-1]
     scratch = [
         pltpu.VMEM((LOCAL, TRACERS, BAND, NLON), f32),
         pltpu.VMEM((LOCAL * TRACERS * BAND, NLON), bf16),
@@ -512,9 +550,14 @@
         pltpu.VMEM((NW, NLAT), bf16),
         pltpu.VMEM((NLAT, NW), bf16),
         pltpu.VMEM((NW, 128), f32),
-        pltpu.VMEM(spread.shape, bf16),
-        pltpu.VMEM(gather.shape, bf16),
-        pltpu.VMEM(home.shape, bf16),
+        pltpu.VMEM(constants[5].shape, bf16),
+        pltpu.VMEM(constants[6].shape, bf16),
+        pltpu.VMEM(constants[7].shape, bf16),
+        pltpu.VMEM(constants[8].shape, bf16),
+        pltpu.VMEM((LOCAL, PATCHES, GROUPS, REACTIONS), bf16),
+        pltpu.VMEM((PATCHES, GROUPS, obs), jnp.int32),
+        pltpu.VMEM((PATCHES, GROUPS, obs), f32),
+        pltpu.VMEM((PATCHES, GROUPS, obs), f32),
         pltpu.VMEM((REACTIONS, BAND, NLON), bf16),
         pltpu.VMEM((REACTIONS, 8, NLON), f32),
         pltpu.VMEM((BLOCKS, LOCAL, TRACERS * BAND, 128), bf16),
@@ -526,47 +569,52 @@
         pltpu.VMEM((GROUPS, 2, BLOCKS, 2, ROWS, 128), bf16),
         pltpu.VMEM((MEMBERS, 16, BLOCKS * 128), f32),
         pltpu.VMEM((ROWS * MEMBERS, 2 * NW), bf16),
-        pltpu.VMEM((GROUPS, 8, 128), f32),
+        pltpu.VMEM((GROUPS, pairs, 128), f32),
+        pltpu.VMEM((GROUPS, pairs, 128), f32),
         pltpu.VMEM((PATCHES, REACTIONS, MEMBERS, 128), f32),
+        pltpu.VMEM((PATCHES, MEMBERS, 128), f32),
+        pltpu.VMEM((PATCHES, MEMBERS, 128), f32),
+        pltpu.VMEM((PATCHES, MEMBERS, 128), f32),
         pltpu.VMEM((PATCHES, ROWS * MEMBERS, PLON), bf16),
         pltpu.VMEM((size, 128), f32),
         pltpu.VMEM((size, 128), f32),
         pltpu.VMEM((size, 128), f32),
         pltpu.VMEM((size, MEMBERS), f32),
         pltpu.VMEM((PATCHES, GROUPS, LOCAL * ROWS, PLON), bf16),
-        pltpu.VMEM((GROUPS, 8, 128), f32),
-        pltpu.VMEM((GROUPS, 8, 128), f32),
-        pltpu.SemaphoreType.DMA((13,)),
+        pltpu.VMEM((GROUPS, pairs, 128), f32),
+        pltpu.VMEM((GROUPS, pairs, 128), f32),
+        pltpu.SemaphoreType.DMA((18,)),
         pltpu.SemaphoreType.DMA((5,)),
         pltpu.SemaphoreType.DMA((5,)),
         pltpu.SemaphoreType.DMA((5,)),
+        pltpu.SemaphoreType.REGULAR,
     ]
     out, mult = pl.pallas_call(
         kernel,
         out_shape=(
             jax.ShapeDtypeStruct((GROUPS, LOCAL * ROWS, NLON), bf16),
-            jax.ShapeDtypeStruct((GROUPS, 8, 128), f32),
+            jax.ShapeDtypeStruct((LOCAL, PATCHES, GROUPS, REACTIONS), bf16),
         ),
-        in_specs=[anywhere, vmem, vmem, vmem, vmem, anywhere] + [anywhere] * 8,
+        in_specs=[anywhere] * (6 + len(constants)),
         out_specs=(anywhere, vmem),
         scratch_shapes=scratch,
         compiler_params=pltpu.CompilerParams(
             collective_id=0, has_side_effects=True, vmem_limit_bytes=60 << 20
         ),
         name="assimilate",
-    )(x, fac, cells, measured, variance, field, forward, inverse, modes, rows, gain, spread, gather, home)
-    analysis = (
-        out.reshape(GROUPS, LOCAL, TRACERS, PLAT, NLON)
-        .transpose(1, 2, 0, 3, 4)
-        .reshape(LOCAL, TRACERS, BAND, NLON)
+    )(
+        x,
+        field,
+        kinetic.transpose(0, 3, 2, 1),
+        cells.transpose(1, 0, 2),
+        measured.transpose(1, 0, 2),
+        variance.transpose(1, 0, 2),
+        *constants,
     )
-    mult = (
-        mult[:, :LOCAL, : PATCHES * REACTIONS]
-        .reshape(GROUPS, LOCAL, PATCHES, REACTIONS)
-        .transpose(1, 3, 0, 2)
-        .astype(bf16)
-    )
-    return analysis, mult
+    analysis = jnp.dot(
+        final, out.reshape(GROUPS * LOCAL * ROWS, NLON), preferred_element_type=f32
+    ).astype(bf16)
+    return analysis.reshape(LOCAL, TRACERS, BAND, NLON), mult.transpose(0, 3, 2, 1)
 
 
 def solution(mesh):

time: 101 us -> 86 us (0.85)
  local copies, waits for them, and re-layouts: 10.2 us -> 0.63 us
  Pallas kernels: 89.2 us -> 81.4 us
  matrix products: 0 us -> 3.06 us
    pallas_call x1, Pallas kernels: 89.2 us -> 81.4 us  [on_device(): pl.pallas_call(kernel, out_shape=(jax.ShapeDtypeStruct((GROUPS, LOCAL * R...]
    unnamed x5, local copies, waits for them, and re-layouts: 5.91 us -> 0.63 us
    dot_general x0 -> x1, matrix products: none -> 3.06 us  [on_device(): jnp.dot(final, out.reshape(GROUPS * LOCAL * ROWS, NLON), preferred_elemen...]
    pallas_call x1 -> x0, local copies, waits for them, and re-layouts: 1.92 us -> none  [on_device(): pl.pallas_call(kernel, out_shape=(jax.ShapeDtypeStruct((GROUPS, LOCAL * R...]
where the time goes in v1:
time: 86 us; the launch traced here: 85.8 us
  Pallas kernels  81.4 us (95%)
  matrix products  3.06 us (4%)
    pallas_call x1, Pallas kernels, on_device(): pl.pallas_call(kernel, out_shape=(jax.ShapeDtypeStruct((GROUPS, LOCAL * R...  81.4 us
    dot_general x1, matrix products, on_device(): jnp.dot(final, out.reshape(GROUPS * LOCAL * ROWS, NLON), preferred_elemen...  3.06 us

profile of v1, /device:TPU:1, one launch (start us, length us, event | category | flops | bytes accessed | tf_op | source)
XLA Modules:
  0.0 85.8 jit_solution(16889441397128979908)
XLA Ops:
  0.6 0.0 copy-start
  0.6 81.4 %assimilate.1 = (bf16[8,48,1536]{2,1,0:T(8,128)(2,1)}, bf16[4,6,8,12]{3,2,1,0:T(8,128)(2,1)}) custom-call(f32[4,4,24,1536]{3,2,1,0:T(8,128)} %x_hbm.1, bf16[12,24,1536]{2,1,0:T(8,128)(2,1)} %field_hbm.1, bf16[4,6,8,12]{3,2,1,0:T(8,128)(2,1)} %bitcast.14, s32[6,8,128]{2,1,0:T(8,128)} %bitcast.15, f32[6,8,128]{2,1,0:T(8,128)} %bitcast.16, ...), custom_call_target="tpu_custom_call" | custom-call | tf_op jit(solution)/shard_map/assimilate/pallas_call | solution.py:592
  82.1 0.0 copy-start.1
  82.1 0.0 copy-done
  82.1 3.1 %convolution_convert_fusion = bf16[1536,384]{0,1:T(8,128)(2,1)} fusion(bf16[384,384]{1,0:T(8,128)(2,1)S(1)} %copy-done, bf16[384,1536]{1,0:T(8,128)(2,1)} %bitcast.11), kind=kOutput, calls=%fused_computation | convolution fusion | flops 453574656 | bytes 2654208 | tf_op jit(solution)/shard_map/dot_general | solution.py:614
  85.1 0.0 copy-done.1
  85.1 0.6 copy.19
Async XLA Ops:
  0.6 81.4 %copy-start = (bf16[384,384]{1,0:T(8,128)(2,1)S(1)}, bf16[384,384]{1,0:T(8,128)(2,1)}, u32[]{:S(2)}) copy-start(bf16[384,384]{1,0:T(8,128)(2,1)} %constant.29.clone) | copy-start | bytes 884740
  82.1 3.1 %copy-start.1 = (bf16[4,6,8,12]{3,2,1,0:T(8,128)(2,1)S(1)}, bf16[4,6,8,12]{3,2,1,0:T(8,128)(2,1)}, u32[]{:S(2)}) copy-start(bf16[4,6,8,12]{3,2,1,0:T(8,128)(2,1)} %get-tuple-element.5) | copy-start | bytes 13828

commit v2 on v1

--- a/solution.py
+++ b/solution.py
@@ -25,7 +25,7 @@
 BANDS = 32
 LOCAL = 4
 BLOCKS = 8
-TOGETHER = 3
+TOGETHER = (3, 3)
 BAND = NLAT // BANDS
 PATCHES = NLON // PLON
 ROWS = TRACERS * PLAT
@@ -105,9 +105,11 @@
     final = np.zeros((index.size, index.size), np.float32)
     final[(et * GROUPS + g) * PLAT + j, index] = 1.0
     b = lambda v: np.asarray(v, np.float32).astype(ml_dtypes.bfloat16)
-    return (
-        (b(forward), b(inverse), b(to_modes), b(to_rows), gain)
-        + (b(spread), b(gather), b(home), b(small)),
+    return (b(forward), b(inverse), b(to_modes), b(to_rows), gain) + (
+        b(spread),
+        b(gather),
+        b(home),
+        b(small),
         b(final),
     )
 
@@ -136,6 +138,7 @@
     gather_hbm,
     home_hbm,
     small_hbm,
+    final_hbm,
     out_hbm,
     mult_out,
     x,
@@ -149,6 +152,7 @@
     gather,
     home,
     small,
+    final,
     fac_raw,
     cells,
     measured,
@@ -167,6 +171,7 @@
     fac,
     fac_in,
     fac_wide,
+    mix,
     log_mean,
     log_spread,
     log_new,
@@ -176,12 +181,16 @@
     projected,
     transform,
     send3,
+    recv3,
+    result,
     mult_send,
     mult_in,
     load_sem,
     local_sem,
     send_sem,
     recv_sem,
+    patch_sem,
+    pair_sem,
     ready,
 ):
     g, b = lax.axis_index("mem"), lax.axis_index("grid")
@@ -209,12 +218,11 @@
         load(inverse_hbm, inverse, 10),
         load(gather_hbm, gather, 11),
         load(home_hbm, home, 12),
+        load(final_hbm, final, 18),
         load(cells_hbm, cells, 15),
         load(measured_hbm, measured, 16),
         load(variance_hbm, variance, 17),
     ]
-    for one in later:
-        one.start()
 
     barrier = pltpu.get_barrier_semaphore()
 
@@ -230,23 +238,6 @@
     for to in bands:
         pl.semaphore_signal(barrier, inc=1, device_id=(g, to), device_id_type=MESH)
 
-    load_x.wait()
-    xb[...] = x[...].reshape(LOCAL * TRACERS * BAND, NLON).astype(bf16)
-    for one in load_forward:
-        one.wait()
-
-    def forward_step(i, carry):
-        value = jnp.dot(xb[...], forward[i], preferred_element_type=f32) * (1.0 / NLON)
-        value = value.astype(bf16).reshape(LOCAL, TRACERS * BAND, 256)
-        send1[2 * i] = value[:, :, :128]
-        send1[2 * i + 1] = value[:, :, 128:]
-        return carry
-
-    lax.fori_loop(0, 4, forward_step, 0)
-    pl.semaphore_wait(barrier, GROUPS + BANDS - 2)
-    for to in groups:
-        pl.semaphore_signal(ready, inc=1, device_id=(to, b), device_id_type=MESH)
-
     def remote(src, dst, i, to):
         return pltpu.make_async_remote_copy(
             src_ref=src,
@@ -260,6 +251,24 @@
     def wait_bytes(ref, sem):
         pltpu.make_async_copy(ref, ref, sem).wait()
 
+    load_x.wait()
+    xb[...] = x[...].reshape(LOCAL * TRACERS * BAND, NLON).astype(bf16)
+    for one in load_forward:
+        one.wait()
+    for one in later:
+        one.start()
+
+    def forward_step(i, carry):
+        value = jnp.dot(xb[...], forward[i], preferred_element_type=f32) * (1.0 / NLON)
+        value = value.astype(bf16).reshape(LOCAL, TRACERS * BAND, 256)
+        send1[2 * i] = value[:, :, :128]
+        send1[2 * i + 1] = value[:, :, 128:]
+        return carry
+
+    lax.fori_loop(0, 4, forward_step, 0)
+    pl.semaphore_wait(barrier, GROUPS + BANDS - 2)
+    for to in groups:
+        pl.semaphore_signal(ready, inc=1, device_id=(to, b), device_id_type=MESH)
     for band in bands:
         h2, z2, c2 = split_grid(band)
         remote(send1.at[z2, h2 * 2 + c2], recv1.at[b], 0, (g, band)).start()
@@ -279,7 +288,7 @@
 
     for one in later:
         one.wait()
-    padded[...] = jnp.zeros(padded.shape, f32)
+    padded[...] = jnp.zeros(padded.shape, bf16)
 
     line_of = lax.broadcasted_iota(jnp.int32, (8, BAND), 0) + g * PLAT
     own_lines = jnp.where(line_of == lax.broadcasted_iota(jnp.int32, (8, BAND), 1), 1.0, 0.0)
@@ -340,69 +349,77 @@
         wide = jnp.dot(spread[...], stacked, preferred_element_type=f32)
         wide = wide.reshape(BANDS, 16, 128).astype(bf16)
         send2[pl.ds(owner * BANDS, BANDS)] = wide[:, :ROWS]
-        for band in bands:
-            remote(
-                send2.at[owner * BANDS + band],
-                recv2.at[g, half, z, core],
-                2,
-                (owner, band),
-            ).start()
-
-        @pl.when(step != 0)
-        def _():
-            remote(
-                send2.at[owner * BANDS + b], recv2.at[g, half, z, core], 2, (owner, b)
-            ).start()
-
+        push(step, owner, 0)
+        return carry
+
+    def push(step, owner, to_core):
+        for a in (1, 0):
+            for dz in ZSTEPS:
+                band = wrap(half + a, 2) * 16 + wrap(z + dz, BLOCKS) * 2 + to_core
+                copy = pltpu.make_async_remote_copy(
+                    src_ref=send2.at[owner * BANDS + band],
+                    dst_ref=recv2.at[g, half, z, core],
+                    send_sem=send_sem.at[2],
+                    recv_sem=pair_sem.at[z // 2],
+                    device_id=(owner, band),
+                    device_id_type=MESH,
+                )
+                if a or dz:
+                    copy.start()
+                else:
+                    pl.when(jnp.logical_or(step != 0, core != to_core))(copy.start)
+
+    def push_rest(step, carry):
+        push(step, wrap(g + step, GROUPS), 1)
+        return carry
+
+    def reaction_step(c, carry):
+        for j in range(PLAT):
+            for h in range(PLON // 128):
+                lanes = pl.ds(pl.multiple_of(c * PLON + h * 128, 128), 128)
+                rates = [fac_wide[c, r] * field_rows[r, j : j + 1, lanes] for r in range(REACTIONS)]
+                for s in range(TRACERS):
+                    outflow = rates[3 * s] + rates[3 * s + 1] + rates[3 * s + 2]
+                    leave = 1.0 / (1.0 + outflow)
+                    mix[c, j, h, s, s] = leave
+                    for t in range(TRACERS):
+                        if t != s:
+                            mix[c, j, h, t, s] = rates[3 * s + (t if t < s else t - 1)] * leave
         return carry
 
     pl.semaphore_wait(ready, GROUPS - 1)
     lax.fori_loop(0, GROUPS, to_owner, 0)
+    lax.fori_loop(0, GROUPS, push_rest, 0)
     own2 = pltpu.make_async_copy(
-        send2.at[g * BANDS + b], recv2.at[g, half, z, core], local_sem.at[2]
+        send2.at[g * BANDS + b], recv2.at[g, half, z, core], pair_sem.at[z // 2]
     )
     own2.start()
-    own2.wait()
-    wait_bytes(send2.at[pl.ds(0, GROUPS * BANDS - 1)], recv_sem.at[2])
-
-    for block in range(BLOCKS):
-        value = recv2[:, :, block, :, :, :].astype(f32).reshape(MEMBERS, ROWS, 128)
-        padded[:, :ROWS, block * 128 : (block + 1) * 128] = value
-
-    def permute(i, carry):
-        lanes = pl.ds(pl.multiple_of(i * 256, 256), 256)
-        value = padded[:, :, lanes].reshape(MEMBERS * 16, 256).astype(bf16)
+    lax.fori_loop(0, PATCHES, reaction_step, 0)
+
+    for i in range(BLOCKS // 2):
+        wait_bytes(recv2.at[:, :, pl.ds(2 * i, 2)], pair_sem.at[i])
+        for block in (2 * i, 2 * i + 1):
+            value = recv2[:, :, block, :, :, :].reshape(MEMBERS, ROWS, 128)
+            padded[:, :ROWS, block * 128 : (block + 1) * 128] = value
+        lanes = slice(i * 256, (i + 1) * 256)
+        value = padded[:, :, lanes].reshape(MEMBERS * 16, 256)
         coefficients[:, lanes] = jnp.dot(
             gather[...], value, preferred_element_type=f32
         ).astype(bf16)
-        return carry
-
-    lax.fori_loop(0, 4, permute, 0)
 
     obs = cells.shape[-1]
 
-    def background_step(i, first):
-        c = first + i
+    def background_step(c):
         smooth = jnp.dot(coefficients[...], inverse[c], preferred_element_type=f32)
         smooth = smooth.reshape(TRACERS, PLAT, MEMBERS, PLON)
         for j in range(PLAT):
             for h in range(PLON // 128):
-                lanes = pl.ds(pl.multiple_of(c * PLON + h * 128, 128), 128)
                 tracers = [smooth[t, j, :, h * 128 : (h + 1) * 128] for t in range(TRACERS)]
-                rates = []
-                for r in range(REACTIONS):
-                    line = field_rows[r, j : j + 1, lanes]
-                    rates.append(fac_wide[c, r] * line)
-                leave, gone = [], []
-                for s in range(TRACERS):
-                    outflow = rates[3 * s] + rates[3 * s + 1] + rates[3 * s + 2]
-                    leave.append(1.0 / (1.0 + outflow))
-                    gone.append(leave[s] * tracers[s])
                 for t in range(TRACERS):
-                    value = gone[t]
+                    value = mix[c, j, h, t, t] * tracers[t]
                     for s in range(TRACERS):
                         if s != t:
-                            value = value + rates[3 * s + (t if t < s else t - 1)] * gone[s]
+                            value = value + mix[c, j, h, t, s] * tracers[s]
                     row = (t * PLAT + j) * MEMBERS
                     background[c, row : row + MEMBERS, h * 128 : (h + 1) * 128] = value.astype(
                         bf16
@@ -423,19 +440,12 @@
         spread_of = predicted - seen_mean
         weight = spread_of * (1.0 / variance[c, pl.ds(g, 1), :])
         innovation = measured[c, pl.ds(g, 1), :] - seen_mean
-        at = pl.ds(pl.multiple_of(i * MEMBERS, MEMBERS), MEMBERS)
+        at = pl.ds(c * MEMBERS, MEMBERS)
         weighted[at, :] = weight
         spread_seen[at, :] = spread_of
         projected[at, :] = jnp.broadcast_to(
             jnp.sum(weight * innovation, axis=1, keepdims=True), (MEMBERS, 128)
         )
-        return first
-
-    size = TOGETHER * MEMBERS
-    block_row = lax.broadcasted_iota(jnp.int32, (size, size), 0)
-    block_col = lax.broadcasted_iota(jnp.int32, (size, size), 1)
-    same = block_row // MEMBERS == block_col // MEMBERS
-    identity = jnp.where(block_row == block_col, 1.0, 0.0)
 
     def halves(value):
         high = value.astype(bf16)
@@ -446,17 +456,23 @@
         dot = functools.partial(jnp.dot, preferred_element_type=f32)
         return dot(a, c) + (dot(a, d) + dot(b, c))
 
-    def solve():
+    def solve(first, last):
+        size = (last - first) * MEMBERS
+        at = slice(first * MEMBERS, last * MEMBERS)
+        block_row = lax.broadcasted_iota(jnp.int32, (size, size), 0)
+        block_col = lax.broadcasted_iota(jnp.int32, (size, size), 1)
+        same = block_row // MEMBERS == block_col // MEMBERS
+        identity = jnp.where(block_row == block_col, 1.0, 0.0)
         outer = lax.dot_general(
-            weighted[...],
-            spread_seen[...],
+            weighted[at, :],
+            spread_seen[at, :],
             (((1,), (1,)), ((), ())),
             precision=HI,
             preferred_element_type=f32,
         )
         outer = jnp.where(same, outer, 0.0)
-        square = jnp.sum(outer * outer, axis=1, keepdims=True).reshape(TOGETHER, MEMBERS, 1)
-        square = jnp.broadcast_to(jnp.sum(square, axis=1, keepdims=True), (TOGETHER, MEMBERS, 1))
+        square = jnp.sum(outer * outer, axis=1, keepdims=True).reshape(last - first, MEMBERS, 1)
+        square = jnp.broadcast_to(jnp.sum(square, axis=1, keepdims=True), (last - first, MEMBERS, 1))
         scale = (MEMBERS - 1.0) + jnp.sqrt(square.reshape(size, 1))
         current = ((MEMBERS - 1.0) * identity + outer) / scale
         root = 1.5 * identity - 0.5 * current
@@ -466,7 +482,7 @@
             if sweep < SWEEPS - 1:
                 current = exact(current, middle)
             root = exact(middle, root)
-        mean_weight = exact(root, exact(root, projected[...])) / scale
+        mean_weight = exact(root, exact(root, projected[at, :])) / scale
         full = jnp.where(same, jnp.sqrt((MEMBERS - 1.0) / scale) * root, 0.0)
         fold = jnp.where(
             lax.rem(lax.broadcasted_iota(jnp.int32, (size, MEMBERS), 0), MEMBERS)
@@ -474,7 +490,7 @@
             1.0,
             0.0,
         )
-        transform[...] = exact(full, fold) + mean_weight[:, :MEMBERS]
+        transform[at, :] = exact(full, fold) + mean_weight[:, :MEMBERS]
 
     def apply(matrix, values, precision=None):
         return lax.dot_general(
@@ -485,9 +501,8 @@
             preferred_element_type=f32,
         )
 
-    def analysis_step(i, first):
-        c = first + i
-        matrix = transform[pl.ds(pl.multiple_of(i * MEMBERS, MEMBERS), MEMBERS), :]
+    def analysis_step(c):
+        matrix = transform[c * MEMBERS : (c + 1) * MEMBERS, :]
         pieces = []
         for k in range(ROWS):
             value = background[c, k * MEMBERS : (k + 1) * MEMBERS, :].astype(f32)
@@ -496,38 +511,69 @@
         analysed = jnp.concatenate(pieces, axis=0)
         sent = jnp.dot(home[...], analysed, preferred_element_type=f32).astype(bf16)
         send3[c] = sent.reshape(GROUPS, LOCAL * ROWS, PLON)
-        lanes = pl.ds(pl.multiple_of(c * PLON, PLON), PLON)
         for to in groups:
-            remote(send3.at[c, to], out_hbm.at[g, :, lanes], 3, (to, b)).start()
-        pltpu.make_async_copy(
-            send3.at[c, g], out_hbm.at[g, :, lanes], local_sem.at[3]
-        ).start()
+            pltpu.make_async_remote_copy(
+                src_ref=send3.at[c, to],
+                dst_ref=recv3.at[c, g],
+                send_sem=send_sem.at[3],
+                recv_sem=patch_sem.at[c],
+                device_id=(to, b),
+                device_id_type=MESH,
+            ).start()
+        recv3[c, g] = send3[c, g]
+
+    def multipliers(c):
+        matrix = transform[c * MEMBERS : (c + 1) * MEMBERS, :]
         log_new[c] = jnp.exp(log_mean[c] + apply(matrix, log_spread[c], HI))
-        return first
-
-    def group_step(i, carry):
-        first = i * TOGETHER
-        lax.fori_loop(0, TOGETHER, background_step, first)
-        solve()
-        lax.fori_loop(0, TOGETHER, analysis_step, first)
-        return carry
-
-    lax.fori_loop(0, PATCHES // TOGETHER, group_step, 0)
-    mult = log_new[...].reshape(PATCHES * MEMBERS, 128).astype(bf16)
-    mult = jnp.dot(small[2], mult, preferred_element_type=f32)
-    mult_send[...] = mult.reshape(GROUPS, pairs, 128)
-    for to in groups:
-        remote(mult_send.at[to], mult_in.at[g], 4, (to, b)).start()
+
+    def finish(first, last):
+        for c in range(first, last):
+            multipliers(c)
+        if last == PATCHES:
+            send_multipliers()
+        for c in range(first, last):
+            analysis_step(c)
+
     own_mult = pltpu.make_async_copy(mult_send.at[g], mult_in.at[g], local_sem.at[4])
-    own_mult.start()
-
+
+    def send_multipliers():
+        mult = log_new[...].reshape(PATCHES * MEMBERS, 128).astype(bf16)
+        mult = jnp.dot(small[2], mult, preferred_element_type=f32)
+        mult_send[...] = mult.reshape(GROUPS, pairs, 128)
+        for to in groups:
+            remote(mult_send.at[to], mult_in.at[g], 4, (to, b)).start()
+        own_mult.start()
+
+    first = 0
+    for count in TOGETHER:
+        last = first + count
+        for c in range(first, last):
+            background_step(c)
+        if first:
+            finish(before, first)
+        solve(first, last)
+        before, first = first, last
+    finish(before, first)
     own_mult.wait()
     wait_bytes(mult_in.at[pl.ds(0, GROUPS - 1)], recv_sem.at[4])
     mult = mult_in[...].reshape(GROUPS * pairs, 128).astype(bf16)
     mult = jnp.dot(small[3], mult, preferred_element_type=f32)
     mult_out[...] = mult.reshape(LOCAL, PATCHES, GROUPS, 128)[..., :REACTIONS].astype(bf16)
-    wait_bytes(send3.at[:, 0], local_sem.at[3])
-    wait_bytes(send3.at[:, pl.ds(0, GROUPS - 1)], recv_sem.at[3])
+
+    def store(c):
+        lanes = pl.ds(pl.multiple_of(c * PLON, PLON), PLON)
+        return pltpu.make_async_copy(result.at[:, lanes], out_hbm.at[:, lanes], local_sem.at[3])
+
+    def final_step(c, carry):
+        wait_bytes(recv3.at[c, pl.ds(0, GROUPS - 1)], patch_sem.at[c])
+        lanes = pl.ds(pl.multiple_of(c * PLON, PLON), PLON)
+        value = recv3[c].reshape(GROUPS * LOCAL * ROWS, PLON)
+        result[:, lanes] = jnp.dot(final[...], value, preferred_element_type=f32).astype(bf16)
+        store(c).start()
+        return carry
+
+    lax.fori_loop(0, PATCHES, final_step, 0)
+    wait_bytes(result, local_sem.at[3])
     wait_bytes(send1.at[pl.ds(0, BLOCKS - 1)], send_sem.at[0])
     wait_bytes(send1.at[0, pl.ds(0, LOCAL - 1)], send_sem.at[0])
     wait_bytes(send2.at[pl.ds(0, GROUPS * BANDS - 1)], send_sem.at[2])
@@ -535,11 +581,27 @@
     wait_bytes(mult_send.at[pl.ds(0, GROUPS - 1)], send_sem.at[4])
 
 
+def keep(values, mult, out, mult_out, held, mult_held, in_sem, out_sem):
+    pieces = [(mult, mult_held, mult_out)]
+    for i in range(8):
+        at = pl.ds(i * 48, 48)
+        pieces.append((values.at[at], held.at[at], out.at[at]))
+    reads = [pltpu.make_async_copy(a, b, in_sem.at[i]) for i, (a, b, _) in enumerate(pieces)]
+    writes = [pltpu.make_async_copy(b, c, out_sem.at[i]) for i, (_, b, c) in enumerate(pieces)]
+    for read in reads:
+        read.start()
+    for read, write in zip(reads, writes):
+        read.wait()
+        write.start()
+    for write in writes:
+        write.wait()
+
+
 def on_device(x, field, kinetic, cells, measured, variance):
-    constants, final = tables()
+    constants = tables()
     anywhere = pl.BlockSpec(memory_space=pl.ANY)
     vmem = pl.BlockSpec(memory_space=pltpu.VMEM)
-    size = TOGETHER * MEMBERS
+    size = PATCHES * MEMBERS
     pairs = LOCAL * PATCHES
     obs = cells.shape[-1]
     scratch = [
@@ -554,6 +616,7 @@
         pltpu.VMEM(constants[6].shape, bf16),
         pltpu.VMEM(constants[7].shape, bf16),
         pltpu.VMEM(constants[8].shape, bf16),
+        pltpu.VMEM(constants[9].shape, bf16),
         pltpu.VMEM((LOCAL, PATCHES, GROUPS, REACTIONS), bf16),
         pltpu.VMEM((PATCHES, GROUPS, obs), jnp.int32),
         pltpu.VMEM((PATCHES, GROUPS, obs), f32),
@@ -567,11 +630,12 @@
         pltpu.VMEM((NW, TRACERS * 128), bf16),
         pltpu.VMEM((GROUPS * BANDS, ROWS, 128), bf16),
         pltpu.VMEM((GROUPS, 2, BLOCKS, 2, ROWS, 128), bf16),
-        pltpu.VMEM((MEMBERS, 16, BLOCKS * 128), f32),
+        pltpu.VMEM((MEMBERS, 16, BLOCKS * 128), bf16),
         pltpu.VMEM((ROWS * MEMBERS, 2 * NW), bf16),
         pltpu.VMEM((GROUPS, pairs, 128), f32),
         pltpu.VMEM((GROUPS, pairs, 128), f32),
         pltpu.VMEM((PATCHES, REACTIONS, MEMBERS, 128), f32),
+        pltpu.VMEM((PATCHES, PLAT, 2, TRACERS, TRACERS, MEMBERS, 128), f32),
         pltpu.VMEM((PATCHES, MEMBERS, 128), f32),
         pltpu.VMEM((PATCHES, MEMBERS, 128), f32),
         pltpu.VMEM((PATCHES, MEMBERS, 128), f32),
@@ -581,18 +645,22 @@
         pltpu.VMEM((size, 128), f32),
         pltpu.VMEM((size, MEMBERS), f32),
         pltpu.VMEM((PATCHES, GROUPS, LOCAL * ROWS, PLON), bf16),
+        pltpu.VMEM((PATCHES, GROUPS, LOCAL * ROWS, PLON), bf16),
+        pltpu.VMEM((LOCAL * TRACERS * BAND, NLON), bf16),
         pltpu.VMEM((GROUPS, pairs, 128), f32),
         pltpu.VMEM((GROUPS, pairs, 128), f32),
-        pltpu.SemaphoreType.DMA((18,)),
+        pltpu.SemaphoreType.DMA((19,)),
         pltpu.SemaphoreType.DMA((5,)),
         pltpu.SemaphoreType.DMA((5,)),
         pltpu.SemaphoreType.DMA((5,)),
+        pltpu.SemaphoreType.DMA((PATCHES,)),
+        pltpu.SemaphoreType.DMA((BLOCKS // 2,)),
         pltpu.SemaphoreType.REGULAR,
     ]
     out, mult = pl.pallas_call(
         kernel,
         out_shape=(
-            jax.ShapeDtypeStruct((GROUPS, LOCAL * ROWS, NLON), bf16),
+            jax.ShapeDtypeStruct((LOCAL * TRACERS * BAND, NLON), bf16),
             jax.ShapeDtypeStruct((LOCAL, PATCHES, GROUPS, REACTIONS), bf16),
         ),
         in_specs=[anywhere] * (6 + len(constants)),
@@ -611,10 +679,24 @@
         variance.transpose(1, 0, 2),
         *constants,
     )
-    analysis = jnp.dot(
-        final, out.reshape(GROUPS * LOCAL * ROWS, NLON), preferred_element_type=f32
-    ).astype(bf16)
-    return analysis.reshape(LOCAL, TRACERS, BAND, NLON), mult.transpose(0, 3, 2, 1)
+    out, mult = pl.pallas_call(
+        keep,
+        out_shape=(
+            jax.ShapeDtypeStruct(out.shape, bf16),
+            jax.ShapeDtypeStruct(mult.shape, bf16),
+        ),
+        in_specs=[anywhere] * 2,
+        out_specs=(anywhere,) * 2,
+        scratch_shapes=[
+            pltpu.VMEM(out.shape, bf16),
+            pltpu.VMEM(mult.shape, bf16),
+            pltpu.SemaphoreType.DMA((9,)),
+            pltpu.SemaphoreType.DMA((9,)),
+        ],
+        compiler_params=pltpu.CompilerParams(vmem_limit_bytes=60 << 20),
+        name="keep",
+    )(out, mult)
+    return out.reshape(LOCAL, TRACERS, BAND, NLON), mult.transpose(0, 3, 2, 1)
 
 
 def solution(mesh):

time: 86 us -> 81.4 us (0.947)
  matrix products: 3.06 us -> 0 us
    dot_general x1 -> x0, matrix products: 3.06 us -> none  [on_device(): jnp.dot(final, out.reshape(GROUPS * LOCAL * ROWS, NLON), preferred_elemen...]
    pallas_call x1 -> x2, Pallas kernels: 81.4 us -> 80.6 us  [the longest x1 78.4 us: on_device(): pl.pallas_call(kernel, out_shape=(jax.ShapeDtypeStruct((LOCAL * TRACERS *...]
where the time goes in v2:
time: 81.4 us; the launch traced here: 81.2 us
  Pallas kernels  80.6 us (99%)
    pallas_call x1, Pallas kernels, on_device(): pl.pallas_call(kernel, out_shape=(jax.ShapeDtypeStruct((LOCAL * TRACERS *...  78.4 us
    pallas_call x1, Pallas kernels, on_device(): pl.pallas_call(keep, out_shape=(jax.ShapeDtypeStruct(out.shape, bf16), ja...  2.19 us

profile of v2, /device:TPU:1, one launch (start us, length us, event | category | flops | bytes accessed | tf_op | source)
XLA Modules:
  0.0 81.2 jit_solution(7063470589680365799)
XLA Ops:
  0.6 78.4 %assimilate.1 = (bf16[384,1536]{1,0:T(8,128)(2,1)}, bf16[4,6,8,12]{3,2,1,0:T(8,128)(2,1)}) custom-call(f32[4,4,24,1536]{3,2,1,0:T(8,128)} %x_hbm.1, bf16[12,24,1536]{2,1,0:T(8,128)(2,1)} %field_hbm.1, bf16[4,6,8,12]{3,2,1,0:T(8,128)(2,1)} %bitcast.6, s32[6,8,128]{2,1,0:T(8,128)} %bitcast.7, f32[6,8,128]{2,1,0:T(8,128)} %bitcast.8, f32[6,8,128]{2,1,0:T(8,128)} %bitcast.9, ...), custom_call_target="tpu_custom_call" | custom-call | tf_op jit(solution)/shard_map/assimilate/pallas_call | solution.py:660
  79.1 2.2 %keep.1 = (bf16[384,1536]{1,0:T(8,128)(2,1)}, bf16[4,6,8,12]{3,2,1,0:T(8,128)(2,1)}) custom-call(bf16[384,1536]{1,0:T(8,128)(2,1)} %get-tuple-element.6.values, bf16[4,6,8,12]{3,2,1,0:T(8,128)(2,1)} %get-tuple-element.7.mult), custom_call_target="tpu_custom_call" | custom-call | tf_op jit(solution)/shard_map/keep/pallas_call | solution.py:682

commit v3 on v2

--- a/solution.py
+++ b/solution.py
@@ -25,7 +25,7 @@
 BANDS = 32
 LOCAL = 4
 BLOCKS = 8
-TOGETHER = (3, 3)
+TOGETHER = (4, 2)
 BAND = NLAT // BANDS
 PATCHES = NLON // PLON
 ROWS = TRACERS * PLAT
@@ -554,25 +554,26 @@
         solve(first, last)
         before, first = first, last
     finish(before, first)
+
+    def store(c):
+        lanes = pl.ds(c * PLON if isinstance(c, int) else pl.multiple_of(c * PLON, PLON), PLON)
+        return pltpu.make_async_copy(result.at[:, lanes], out_hbm.at[:, lanes], local_sem.at[3])
+
+    def final_step(c, carry):
+        wait_bytes(recv3.at[c, pl.ds(0, GROUPS - 1)], patch_sem.at[c])
+        lanes = pl.ds(c * PLON if isinstance(c, int) else pl.multiple_of(c * PLON, PLON), PLON)
+        value = recv3[c].reshape(GROUPS * LOCAL * ROWS, PLON)
+        result[:, lanes] = jnp.dot(final[...], value, preferred_element_type=f32).astype(bf16)
+        store(c).start()
+        return carry
+
+    lax.fori_loop(0, PATCHES - 1, final_step, 0)
     own_mult.wait()
     wait_bytes(mult_in.at[pl.ds(0, GROUPS - 1)], recv_sem.at[4])
     mult = mult_in[...].reshape(GROUPS * pairs, 128).astype(bf16)
     mult = jnp.dot(small[3], mult, preferred_element_type=f32)
     mult_out[...] = mult.reshape(LOCAL, PATCHES, GROUPS, 128)[..., :REACTIONS].astype(bf16)
-
-    def store(c):
-        lanes = pl.ds(pl.multiple_of(c * PLON, PLON), PLON)
-        return pltpu.make_async_copy(result.at[:, lanes], out_hbm.at[:, lanes], local_sem.at[3])
-
-    def final_step(c, carry):
-        wait_bytes(recv3.at[c, pl.ds(0, GROUPS - 1)], patch_sem.at[c])
-        lanes = pl.ds(pl.multiple_of(c * PLON, PLON), PLON)
-        value = recv3[c].reshape(GROUPS * LOCAL * ROWS, PLON)
-        result[:, lanes] = jnp.dot(final[...], value, preferred_element_type=f32).astype(bf16)
-        store(c).start()
-        return carry
-
-    lax.fori_loop(0, PATCHES, final_step, 0)
+    final_step(PATCHES - 1, 0)
     wait_bytes(result, local_sem.at[3])
     wait_bytes(send1.at[pl.ds(0, BLOCKS - 1)], send_sem.at[0])
     wait_bytes(send1.at[0, pl.ds(0, LOCAL - 1)], send_sem.at[0])

time: 81.4 us -> 81.1 us (level)
  no operation moved by 1% of the time
where the time goes in v3:
time: 81.1 us; the launch traced here: 80.9 us
  Pallas kernels  80.3 us (99%)
    pallas_call x1, Pallas kernels, on_device(): pl.pallas_call(kernel, out_shape=(jax.ShapeDtypeStruct((LOCAL * TRACERS *...  78.1 us
    pallas_call x1, Pallas kernels, on_device(): pl.pallas_call(keep, out_shape=(jax.ShapeDtypeStruct(out.shape, bf16), ja...  2.19 us

profile of v3, /device:TPU:1, one launch (start us, length us, event | category | flops | bytes accessed | tf_op | source)
XLA Modules:
  0.0 80.9 jit_solution(11187228079725886931)
XLA Ops:
  0.6 78.1 %assimilate.1 = (bf16[384,1536]{1,0:T(8,128)(2,1)}, bf16[4,6,8,12]{3,2,1,0:T(8,128)(2,1)}) custom-call(f32[4,4,24,1536]{3,2,1,0:T(8,128)} %x_hbm.1, bf16[12,24,1536]{2,1,0:T(8,128)(2,1)} %field_hbm.1, bf16[4,6,8,12]{3,2,1,0:T(8,128)(2,1)} %bitcast.6, s32[6,8,128]{2,1,0:T(8,128)} %bitcast.7, f32[6,8,128]{2,1,0:T(8,128)} %bitcast.8, f32[6,8,128]{2,1,0:T(8,128)} %bitcast.9, ...), custom_call_target="tpu_custom_call" | custom-call | tf_op jit(solution)/shard_map/assimilate/pallas_call | solution.py:661
  78.8 2.2 %keep.1 = (bf16[384,1536]{1,0:T(8,128)(2,1)}, bf16[4,6,8,12]{3,2,1,0:T(8,128)(2,1)}) custom-call(bf16[384,1536]{1,0:T(8,128)(2,1)} %get-tuple-element.6.values, bf16[4,6,8,12]{3,2,1,0:T(8,128)(2,1)} %get-tuple-element.7.mult), custom_call_target="tpu_custom_call" | custom-call | tf_op jit(solution)/shard_map/keep/pallas_call | solution.py:683
